TPU v7x, 32 devices: a whole 2x2x4 slice. The times are simulated.
32 devices in a mesh: groups: 2 (over y), expert: 16 (over z, x, core).
Axes of the slice: x: 2, y: 2, z: 4, core: 2. Of those that a mesh axis runs over, the one named last changes fastest.
Arguments:
- queries: bfloat16 [192, 6144], P(('groups', 'expert')), parts along dimension 0, may hold values from -8 to 8
- tree_key_value: bfloat16 [192, 2, 1024], P(('groups', 'expert')), parts along dimension 0, may hold values from -6 to 6
- key_value_cache: bfloat16 [32, 2, 512, 1024], P(('groups', 'expert')), parts along dimension 0, may hold values from -8 to 8
- lengths: int32 [32], P(('groups', 'expert')), parts along dimension 0, may hold values from 128 to 512, as said below
- parents: int32 [192], P(('groups', 'expert')), parts along dimension 0, may hold values from 0 to 4, as said below
- residual: bfloat16 [192, 6144], P(('groups', 'expert')), parts along dimension 0, may hold values from -6 to 6
- ffn_gain: bfloat16 [6144], replicated, may hold values from 0.099609375 to 1.8984375
- router: bfloat16 [6144, 4], replicated, may hold values from -0.078125 to 0.078125
- routes: int32 [192, 2], P(('groups', 'expert')), parts along dimension 0, may hold values from 0 to 3, all different within a row; in each aligned block of 6 rows (0 to 5, 6 to 11, ...) at most 4 rows name the same one
- gate_weight: bfloat16 [6144, 32768], P(None, 'expert'), may hold values from -0.078125 to 0.078125
- up_weight: bfloat16 [6144, 32768], P(None, 'expert'), may hold values from -0.078125 to 0.078125
- down_weight: bfloat16 [32768, 6144], P('expert'), may hold values from -0.0625 to 0.0625
- accepted: int32 [32], P(('groups', 'expert')), parts along dimension 0, may hold values from 0 to 5
- next_embed: bfloat16 [32, 6144], P(('groups', 'expert')), parts along dimension 0, may hold values from -6 to 6
- draft_fc: bfloat16 [12288, 6144], P('expert'), may hold values from -0.0546875 to 0.0546875
Outputs:
- layer_out: bfloat16 [192, 6144], P(('groups', 'expert')), parts along dimension 0
- draft_out: bfloat16 [32, 6144], P(('groups', 'expert')), parts along dimension 0
There are 2 independent parts, one for each index of `groups`. A program takes and returns all parts, laid end to end along the dimension named above; an argument that names none is the same for every part. Nothing has to cross between parts.
Inputs may be any that keep to these rules, and one draw needn't show every extreme that they name: `lengths`: both ends are reached by some request. `parents`: entry i of a request's 6 entries names an earlier node as its parent; entry 0, the root, names itself. `routes`: among the rows of one device no expert is named more than 4 times, a bound that some block reaches.
All inputs are finite; a program needn't handle non-finite values.
Results may differ from a plain program's by a relative error of at most 0.0051.
Values may be sent and summed in bfloat16 or wider, within the bound.
A program may use at most 128 MiB of HBM per device.

v0:
```python
import jax
import jax.numpy as jnp
from jax import lax
from jax.sharding import PartitionSpec as P

QUERY_HEADS = 48
KEY_VALUE_HEADS = 8
HEAD_SIZE = 128
EXPERTS = 4
TREE_NODES = 6
CACHE_SLOTS = 512
CAP = 4


EPSILON = 1e-05


def ancestors(parent_ids):
    node_ids = jnp.arange(TREE_NODES, dtype=jnp.int32)
    parent_map = (parent_ids[:, :, None] == node_ids[None, None, :]).astype(jnp.float32)
    current = jnp.broadcast_to(jnp.eye(TREE_NODES, dtype=jnp.float32), parent_map.shape)
    reached = current
    for repeat in range(TREE_NODES):
        current = jnp.einsum("rij,rjk->rik", current, parent_map, precision=lax.Precision.HIGHEST)
        reached = reached + current
    return reached > 0.5


def attention(queries, tree_key_value, key_value_cache, lengths, parents):
    request_total = lengths.shape[0]
    query_head_count = queries.reshape(
        request_total, TREE_NODES, KEY_VALUE_HEADS, QUERY_HEADS // KEY_VALUE_HEADS, HEAD_SIZE
    )
    cached_key_rows = key_value_cache[:, 0].reshape(
        request_total, CACHE_SLOTS, KEY_VALUE_HEADS, HEAD_SIZE
    )
    cached_value_rows = key_value_cache[:, 1].reshape(
        request_total, CACHE_SLOTS, KEY_VALUE_HEADS, HEAD_SIZE
    )
    tree_key_rows = tree_key_value[:, 0].reshape(
        request_total, TREE_NODES, KEY_VALUE_HEADS, HEAD_SIZE
    )
    tree_value_rows = tree_key_value[:, 1].reshape(
        request_total, TREE_NODES, KEY_VALUE_HEADS, HEAD_SIZE
    )
    score_scale = HEAD_SIZE ** (-0.5)
    cache_scores = (
        jnp.einsum(
            "rtgqd,rlgd->rgtql",
            query_head_count,
            cached_key_rows,
            preferred_element_type=jnp.float32,
        )
        * score_scale
    )
    tree_scores = (
        jnp.einsum(
            "rtgqd,rugd->rgtqu", query_head_count, tree_key_rows, preferred_element_type=jnp.float32
        )
        * score_scale
    )
    visible = jnp.arange(CACHE_SLOTS, dtype=jnp.int32)[None, :] < lengths[:, None]
    related = ancestors(parents.reshape(request_total, TREE_NODES))
    cache_scores = jnp.where(visible[:, None, None, None, :], cache_scores, -1e30)
    tree_scores = jnp.where(related[:, None, :, None, :], tree_scores, -1e30)
    row_peak = jnp.maximum(jnp.max(cache_scores, axis=-1), jnp.max(tree_scores, axis=-1))[..., None]
    cache_exp = jnp.exp(cache_scores - row_peak)
    tree_exp = jnp.exp(tree_scores - row_peak)
    denominator = (jnp.sum(cache_exp, axis=-1) + jnp.sum(tree_exp, axis=-1))[..., None]
    cache_weights = (cache_exp / denominator).astype(jnp.bfloat16)
    tree_weights = (tree_exp / denominator).astype(jnp.bfloat16)
    context = jnp.einsum(
        "rgtql,rlgd->rtgqd", cache_weights, cached_value_rows, preferred_element_type=jnp.float32
    ) + jnp.einsum(
        "rgtqu,rugd->rtgqd", tree_weights, tree_value_rows, preferred_element_type=jnp.float32
    )
    return context.reshape(request_total * TREE_NODES, QUERY_HEADS * HEAD_SIZE)


def expert_rows(rows, gate_weight, up_weight, down_weight):
    gate_val = jnp.dot(rows, gate_weight, preferred_element_type=jnp.float32)
    up_val = jnp.dot(rows, up_weight, preferred_element_type=jnp.float32)
    activation = (jax.nn.silu(gate_val) * up_val).astype(jnp.bfloat16)
    return jnp.dot(activation, down_weight, preferred_element_type=jnp.float32).astype(jnp.bfloat16)


def per_device(
    queries,
    tree_key_value,
    key_value_cache,
    lengths,
    parents,
    residual,
    ffn_gain,
    router,
    routes,
    gate_weight,
    up_weight,
    down_weight,
    accepted,
    next_embed,
    draft_fc,
):
    devices = lax.axis_size("expert")
    group_size = devices // EXPERTS
    context = attention(queries, tree_key_value, key_value_cache, lengths, parents)
    hidden_state = residual.astype(jnp.float32) + context
    normed = (
        hidden_state
        * lax.rsqrt(jnp.mean(hidden_state * hidden_state, axis=-1, keepdims=True) + EPSILON)
        * ffn_gain.astype(jnp.float32)
    ).astype(jnp.bfloat16)
    tokens_here, model_width = normed.shape
    logits = jnp.dot(normed, router, preferred_element_type=jnp.float32)
    expert_ids = jnp.arange(EXPERTS, dtype=jnp.int32)
    first_hit = (routes[:, 0:1] == expert_ids[None, :]).astype(jnp.float32)
    second_hit = (routes[:, 1:2] == expert_ids[None, :]).astype(jnp.float32)
    first_logit = jnp.sum(logits * first_hit, axis=-1)
    second_logit = jnp.sum(logits * second_hit, axis=-1)
    first_share = jax.nn.sigmoid(first_logit - second_logit)
    mixing = first_share[:, None] * first_hit + (1.0 - first_share)[:, None] * second_hit
    hit_table = first_hit + second_hit
    slot_rank = jnp.cumsum(hit_table, axis=0) - 1.0
    slot_ids = jnp.arange(CAP, dtype=jnp.float32)
    placing = hit_table.T[:, None, :] * (slot_rank.T[:, None, :] == slot_ids[None, :, None]).astype(
        jnp.float32
    )
    packed = jnp.einsum(
        "ect,td->ecd", placing.astype(jnp.bfloat16), normed, preferred_element_type=jnp.float32
    ).astype(jnp.bfloat16)
    outgoing = jnp.broadcast_to(packed[:, None], (EXPERTS, group_size, CAP, model_width)).reshape(
        devices, CAP, model_width
    )
    received = lax.all_to_all(outgoing, "expert", split_axis=0, concat_axis=0, tiled=True)
    flat_rows = received.reshape(-1, model_width)
    computed = expert_rows(flat_rows, gate_weight, up_weight, down_weight).reshape(received.shape)
    returned = lax.all_to_all(computed, "expert", split_axis=0, concat_axis=0, tiled=True)
    grouped = jnp.sum(
        returned.reshape(EXPERTS, group_size, CAP, model_width), axis=1, dtype=jnp.float32
    )
    weighted = placing * mixing.T[:, None, :]
    expert_sum = jnp.einsum("ect,ecd->td", weighted, grouped, precision=lax.Precision.HIGHEST)
    layer_out = (hidden_state + expert_sum).astype(jnp.bfloat16)
    request_total = lengths.shape[0]
    picker = (accepted[:, None] == jnp.arange(TREE_NODES, dtype=jnp.int32)[None, :]).astype(
        jnp.bfloat16
    )
    picked = jnp.einsum(
        "rt,rtd->rd",
        picker,
        layer_out.reshape(request_total, TREE_NODES, model_width),
        preferred_element_type=jnp.float32,
    ).astype(jnp.bfloat16)
    draft_in = jnp.concatenate([picked, next_embed], axis=1)
    columns_in = lax.all_to_all(draft_in, "expert", split_axis=1, concat_axis=0, tiled=True)
    draft_out = lax.psum_scatter(
        jnp.dot(columns_in, draft_fc, preferred_element_type=jnp.float32),
        "expert",
        scatter_dimension=0,
        tiled=True,
    ).astype(jnp.bfloat16)
    return (layer_out, draft_out)


def solution(mesh):
    return jax.shard_map(
        per_device,
        mesh=mesh,
        in_specs=(
            P(("groups", "expert"), None),
            P(("groups", "expert"), None, None),
            P(("groups", "expert"), None, None, None),
            P(("groups", "expert")),
            P(("groups", "expert")),
            P(("groups", "expert"), None),
            P(),
            P(),
            P(("groups", "expert"), None),
            P(None, "expert"),
            P(None, "expert"),
            P("expert", None),
            P(("groups", "expert")),
            P(("groups", "expert"), None),
            P("expert", None),
        ),
        out_specs=(P(("groups", "expert"), None), P(("groups", "expert"), None)),
        check_vma=False,
    )
```

profile of v0, /device:TPU:0, one launch (start us, length us, event | category | flops | bytes accessed | tf_op | source)
XLA Modules:
  0.0 183.0 jit_solution(12144676580039937745)
XLA Ops:
  0.6 0.9 fusion.36
  1.5 0.8 fusion.35
  2.3 0.8 fusion.34
  3.2 0.8 fusion.33
  4.0 0.8 fusion.32
  4.9 0.8 fusion.6
  5.7 1.0 reshape.375
  6.7 0.9 slice_reduce_fusion
  7.7 1.7 fusion.50
  9.4 0.5 copy.71
  10.6 0.6 fusion.52
  12.0 0.5 copy.72
  12.8 0.5 fusion.5
  13.4 1.1 multiply_reduce_fusion
  14.5 0.7 convert_element_type.79
  15.2 0.8 slice_bitcast_fusion.1
  15.9 1.0 multiply_convert_fusion
  17.9 27.3 %all_to_all.23 = bf16[16,4,6144]{2,1,0:T(4,128)(2,1)S(1)} all-to-all(bf16[16,4,6144]{2,1,0:T(4,128)(2,1)S(1)} %bitcast.82), channel_id=1, replica_groups=mesh['groups'=2,'expert'=16] {'expert'}, dimensions={0} | all-to-all | bytes 1572864 | tf_op jit(solution)/shard_map/all_to_all | solution.py:134
  45.3 10.5 %fusion.53 = f32[64,2048]{1,0:T(8,128)S(1)} fusion(bf16[64,6144]{1,0:T(8,128)(2,1)S(1)} %reshape.382, bf16[6144,2048]{1,0:T(8,128)(2,1)} %param.24), kind=kOutput, calls=%fused_computation.97 | convolution fusion | flops 1610612736 | bytes 26476544 | tf_op jit(solution)/shard_map/dot_general | solution.py:81
  55.9 20.0 %convolution_convert_fusion = bf16[64,6144]{1,0:T(8,128)(2,1)S(1)} fusion(bf16[2048,6144]{1,0:T(8,128)(2,1)} %param.26, bf16[64,6144]{1,0:T(8,128)(2,1)S(1)} %reshape.382, bf16[6144,2048]{1,0:T(8,128)(2,1)} %param.25, f32[64,2048]{1,0:T(8,128)S(1)} %fusion.53), kind=kOutput, calls=%fused_computation | convolution fusion | flops 3222405120 | bytes 52428800 | tf_op jit(solution)/shard_map/dot_general | solution.py:84
  75.9 1.2 reshape.383
  77.0 3.9 %all-to-all-start.1 = ((bf16[16,4,6144]{2,1,0:T(4,128)(2,1)}), bf16[16,4,6144]{2,1,0:T(4,128)(2,1)S(1)}, u32[]{:S(2)}, u32[]{:S(2)}) async-start(bf16[16,4,6144]{2,1,0:T(4,128)(2,1)} %reshape.383), calls=%async_computation.1 | async-start | bytes 1572864 | tf_op jit(solution)/shard_map/all_to_all | solution.py:137
  81.7 17.9 %all-to-all-done.1 = bf16[16,4,6144]{2,1,0:T(4,128)(2,1)S(1)} async-done(((bf16[16,4,6144]{2,1,0:T(4,128)(2,1)}), bf16[16,4,6144]{2,1,0:T(4,128)(2,1)S(1)}, u32[]{:S(2)}, u32[]{:S(2)}) %all-to-all-start.1) | async-done | bytes 786464 | tf_op jit(solution)/shard_map/all_to_all | solution.py:137
  100.0 0.9 fusion.1
  101.7 0.8 reduce.13
  102.5 0.6 reshape.397
  103.1 5.4 %all-to-all-start.2 = ((bf16[16,2,384]{2,1,0:T(2,128)(2,1)}), bf16[16,2,384]{2,1,0:T(2,128)(2,1)S(1)}, u32[]{:S(2)}, u32[]{:S(2)}) async-start(bf16[16,2,384]{2,1,0:T(2,128)(2,1)} %reshape.397), calls=%async_computation.2 | async-start | bytes 49152 | tf_op jit(solution)/shard_map/all_to_all | solution.py:155
  108.5 0.7 dynamic-slice
  109.2 5.9 %all-to-all-done.2 = bf16[16,2,384]{2,1,0:T(2,128)(2,1)S(1)} async-done(((bf16[16,2,384]{2,1,0:T(2,128)(2,1)}), bf16[16,2,384]{2,1,0:T(2,128)(2,1)S(1)}, u32[]{:S(2)}, u32[]{:S(2)}) %all-to-all-start.2) | async-done | bytes 24608 | tf_op jit(solution)/shard_map/all_to_all | solution.py:155
  115.1 5.0 %fusion.22 = f32[16,6144]{1,0:T(8,128)S(1)} fusion(bf16[768,6144]{1,0:T(8,128)(2,1)} %param.29, bf16[1,16,768]{2,0,1:T(2,128)(2,1)S(1)} %bitcast.85), kind=kOutput, calls=%fused_computation.39 | convolution fusion | flops 150994944 | bytes 9854976 | tf_op jit(solution)/shard_map/dot_general | solution.py:157
  120.1 61.5 %all-reduce.2 = bf16[16,6144]{1,0:T(8,128)(2,1)S(1)} all-reduce(f32[16,6144]{1,0:T(8,128)S(1)} %fusion.22), channel_id=2, replica_groups=mesh['groups'=2,'expert'=16] {'expert'}, use_global_device_ids=true, to_apply=%region_9.10.clone | all-reduce | flops 98304 | bytes 589824
  181.6 1.3 dynamic-slice_convert_fusion
  (43 shorter events, 3.5 us)
Async XLA Ops:
  0.6 16.3 %copy-start = (bf16[6144,4]{0,1:T(4,128)(2,1)S(1)}, bf16[6144,4]{0,1:T(4,128)(2,1)}, u32[]{:S(2)}) copy-start(bf16[6144,4]{0,1:T(4,128)(2,1)} %param.22) | copy-start | bytes 147460
  55.8 25.8 %copy-start.4 = (bf16[1,6144]{1,0:T(2,128)(2,1)S(1)}, bf16[1,6144]{1,0:T(2,128)(2,1)}, u32[]{:S(2)}) copy-start(bf16[1,6144]{1,0:T(2,128)(2,1)} %param.28) | copy-start | bytes 36868
  55.8 44.2 %copy-start.2 = (bf16[6,6144]{1,0:T(8,128)(2,1)S(1)}, bf16[6,6144]{1,0:T(8,128)(2,1)}, u32[]{:S(2)}) copy-start(bf16[6,6144]{1,0:T(8,128)(2,1)} %param.20) | copy-start | bytes 221188
  55.9 52.7 %copy-start.5 = (u32[32]{0:T(128)S(1)}, u32[32]{0:T(128)}, u32[]{:S(2)}) copy-start(u32[32]{0:T(128)} %constant.42) | copy-start | bytes 388
  55.9 127.1 %copy-start.1 = (bf16[6144,4]{0,1:T(4,128)(2,1)S(1)}, bf16[6144,4]{0,1:T(4,128)(2,1)}, u32[]{:S(2)}) copy-start(bf16[6144,4]{0,1:T(4,128)(2,1)} %param.22) | copy-start | bytes 147460
  77.0 22.6 %all-to-all-start.1 = ((bf16[16,4,6144]{2,1,0:T(4,128)(2,1)}), bf16[16,4,6144]{2,1,0:T(4,128)(2,1)S(1)}, u32[]{:S(2)}, u32[]{:S(2)}) async-start(bf16[16,4,6144]{2,1,0:T(4,128)(2,1)} %reshape.383), calls=%async_computation.1 | async-start | bytes 1572864 | tf_op jit(solution)/shard_map/all_to_all | solution.py:137
  100.9 82.0 %copy-start.3 = (bf16[6,6144]{1,0:T(8,128)(2,1)}, bf16[6,6144]{1,0:T(8,128)(2,1)S(1)}, u32[]{:S(2)}) copy-start(bf16[6,6144]{1,0:T(8,128)(2,1)S(1)} %fusion.1) | copy-start | bytes 221188
  103.1 12.0 %all-to-all-start.2 = ((bf16[16,2,384]{2,1,0:T(2,128)(2,1)}), bf16[16,2,384]{2,1,0:T(2,128)(2,1)S(1)}, u32[]{:S(2)}, u32[]{:S(2)}) async-start(bf16[16,2,384]{2,1,0:T(2,128)(2,1)} %reshape.397), calls=%async_computation.2 | async-start | bytes 49152 | tf_op jit(solution)/shard_map/all_to_all | solution.py:155
where the time goes:
time: 184 us; the launch traced here: 183 us
  blocking collectives  88.8 us (48%)
  matrix products  43.7 us (24%)
  waiting for transfers between devices  23.8 us (13%)
  local copies, waits for them, and re-layouts  10.5 us (6%)
  starting transfers between devices  9.31 us (5%)
  other arithmetic  4.61 us (3%)
  between operations  2.26 us (1%)
    unnamed x1, blocking collectives  61.5 us
    all_to_all x1, blocking collectives, per_device(): lax.all_to_all(outgoing, 'expert', split_axis=0, concat_axis=0, tiled=True)  27.3 us
    dot_general x1, matrix products, expert_rows(): jnp.dot(activation, down_weight, preferred_element_type=jnp.float32)  20 us
    all_to_all x1, waiting for transfers between devices, per_device(): lax.all_to_all(computed, 'expert', split_axis=0, concat_axis=0, tiled=True)  17.9 us
    dot_general x1, matrix products, expert_rows(): gate_val = jnp.dot(rows, gate_weight, preferred_element_type=jnp.float32)  10.5 us
    all_to_all x1, waiting for transfers between devices, per_device(): lax.all_to_all(draft_in, 'expert', split_axis=1, concat_axis=0, tiled=True)  5.89 us
    all_to_all x1, starting transfers between devices, per_device(): lax.all_to_all(draft_in, 'expert', split_axis=1, concat_axis=0, tiled=True)  5.38 us
    dot_general x6, matrix products, ancestors(): jnp.einsum('rij,rjk->rik', current, parent_map, precision=lax.Precision.H...  5.08 us
  transfers between devices with their start and end apart: 2, of which 2 were waited for; matrix products, arithmetic and copies ran while one was open for 0% of the time, Pallas kernels for 0%

commit v1 on v0

--- a/solution.py
+++ b/solution.py
@@ -1,6 +1,10 @@
+import functools
+
 import jax
 import jax.numpy as jnp
 from jax import lax
+from jax.experimental import pallas as pl
+from jax.experimental.pallas import tpu as pltpu
 from jax.sharding import PartitionSpec as P
 
 QUERY_HEADS = 48
@@ -77,11 +81,374 @@
     return context.reshape(request_total * TREE_NODES, QUERY_HEADS * HEAD_SIZE)
 
 
-def expert_rows(rows, gate_weight, up_weight, down_weight):
-    gate_val = jnp.dot(rows, gate_weight, preferred_element_type=jnp.float32)
-    up_val = jnp.dot(rows, up_weight, preferred_element_type=jnp.float32)
-    activation = (jax.nn.silu(gate_val) * up_val).astype(jnp.bfloat16)
-    return jnp.dot(activation, down_weight, preferred_element_type=jnp.float32).astype(jnp.bfloat16)
+VMEM_LIMIT = 66_000_000
+
+
+def greet(n, me):
+    barrier = pltpu.get_barrier_semaphore()
+
+    def hello(k, carry):
+        pl.semaphore_signal(barrier, inc=1, device_id={"expert": lax.rem(me + k, n)})
+        return carry
+
+    lax.fori_loop(1, n, hello, 0)
+    pl.semaphore_wait(barrier, n - 1)
+
+
+def push(src, dst, send_sem, recv_sem, peer):
+    return pltpu.make_async_remote_copy(
+        src_ref=src,
+        dst_ref=dst,
+        send_sem=send_sem,
+        recv_sem=recv_sem,
+        device_id={"expert": peer},
+        device_id_type=pl.DeviceIdType.MESH,
+    )
+
+
+def moe_kernel(
+    n,
+    group_size,
+    pair_slots,
+    down_slots,
+    packed,
+    gate_hbm,
+    up_hbm,
+    down_hbm,
+    grouped,
+    gate_buf,
+    up_buf,
+    down_buf,
+    arrived,
+    rows_wide,
+    rows,
+    activation,
+    result,
+    leaving,
+    returned,
+    pair_sem,
+    down_sem,
+    out_sem,
+    in_sem,
+    back_out_sem,
+    back_in_sem,
+    own_sem,
+):
+    me = lax.axis_index("expert")
+    width = gate_hbm.shape[1]
+    chunk = gate_buf.shape[2]
+    pair_count = width // chunk
+    piece = down_buf.shape[2]
+    piece_count = down_hbm.shape[1] // piece
+
+    def pair_copies(i):
+        slot = lax.rem(i, pair_slots)
+        cols = pl.ds(pl.multiple_of(i * chunk, chunk), chunk)
+        return (
+            pltpu.make_async_copy(gate_hbm.at[:, cols], gate_buf.at[slot], pair_sem.at[0, slot]),
+            pltpu.make_async_copy(up_hbm.at[:, cols], up_buf.at[slot], pair_sem.at[1, slot]),
+        )
+
+    def down_copy(i):
+        slot = lax.rem(i, down_slots)
+        cols = pl.ds(pl.multiple_of(i * piece, piece), piece)
+        return pltpu.make_async_copy(down_hbm.at[:, cols], down_buf.at[slot], down_sem.at[slot])
+
+    def start_pair(i, carry):
+        for copy in pair_copies(i):
+            copy.start()
+        return carry
+
+    def start_down(i, carry):
+        down_copy(i).start()
+        return carry
+
+    lax.fori_loop(0, pair_slots, start_pair, 0)
+    greet(n, me)
+
+    def dispatch(k, carry):
+        peer = lax.rem(me + k, n)
+        push(
+            packed.at[peer // group_size], arrived.at[me], out_sem.at[peer], in_sem.at[me], peer
+        ).start()
+        return carry
+
+    lax.fori_loop(1, n, dispatch, 0)
+    own = pltpu.make_async_copy(packed.at[me // group_size], arrived.at[me], own_sem)
+    own.start()
+    lax.fori_loop(0, down_slots, start_down, 0)
+    own.wait()
+
+    def take(k, carry):
+        source = lax.rem(me + n - k, n)
+        push(
+            packed.at[0], arrived.at[source], out_sem.at[source], in_sem.at[source], source
+        ).wait_recv()
+        return carry
+
+    lax.fori_loop(1, n, take, 0)
+
+    def both(pair):
+        return pl.ds(pl.multiple_of(pair * 2 * CAP, 2 * CAP), 2 * CAP)
+
+    def widen(pair, carry):
+        rows_wide[both(pair), :] = jnp.concatenate(
+            [arrived[2 * pair].astype(jnp.float32), arrived[2 * pair + 1].astype(jnp.float32)],
+            axis=0,
+        )
+        return carry
+
+    lax.fori_loop(0, n // 2, widen, 0)
+    rows[...] = rows_wide[...].astype(jnp.bfloat16)
+
+    def pair_step(i, carry):
+        slot = lax.rem(i, pair_slots)
+        for copy in pair_copies(i):
+            copy.wait()
+        gate_val = jnp.dot(rows[...], gate_buf[slot], preferred_element_type=jnp.float32)
+        up_val = jnp.dot(rows[...], up_buf[slot], preferred_element_type=jnp.float32)
+        cols = pl.ds(pl.multiple_of(i * chunk, chunk), chunk)
+        activation[:, cols] = (jax.nn.silu(gate_val) * up_val).astype(jnp.bfloat16)
+
+        @pl.when(i + pair_slots < pair_count)
+        def _():
+            start_pair(i + pair_slots, 0)
+
+        return carry
+
+    lax.fori_loop(0, pair_count, pair_step, 0)
+
+    def down_step(i, carry):
+        slot = lax.rem(i, down_slots)
+        down_copy(i).wait()
+        result[...] = jnp.dot(
+            activation[...], down_buf[slot], preferred_element_type=jnp.float32
+        )
+
+        @pl.when(i + down_slots < piece_count)
+        def _():
+            start_down(i + down_slots, 0)
+
+        def narrow(pair, inner):
+            block = result[both(pair), :]
+            leaving[2 * pair, i] = block[:CAP].astype(jnp.bfloat16)
+            leaving[2 * pair + 1, i] = block[CAP:].astype(jnp.bfloat16)
+            return inner
+
+        lax.fori_loop(0, n // 2, narrow, 0)
+
+        def send_back(k, inner):
+            peer = lax.rem(me + k, n)
+            push(
+                leaving.at[peer, i],
+                returned.at[me, i],
+                back_out_sem.at[peer],
+                back_in_sem.at[me],
+                peer,
+            ).start()
+            return inner
+
+        lax.fori_loop(1, n, send_back, 0)
+        return carry
+
+    lax.fori_loop(0, piece_count, down_step, 0)
+    returned[me] = leaving[me]
+
+    def drain(k, carry):
+        peer = lax.rem(me + n - k, n)
+        push(
+            leaving.at[peer], returned.at[peer], back_out_sem.at[peer], back_in_sem.at[peer], peer
+        ).wait()
+        push(
+            packed.at[0], arrived.at[peer], out_sem.at[peer], in_sem.at[peer], peer
+        ).wait_send()
+        return carry
+
+    lax.fori_loop(1, n, drain, 0)
+
+    def gather(expert, carry):
+        for i in range(piece_count):
+
+            def add(member, total):
+                return total + returned[expert * group_size + member, i].astype(jnp.float32)
+
+            grouped[expert, :, i * piece : (i + 1) * piece] = lax.fori_loop(
+                0, group_size, add, jnp.zeros((CAP, piece), jnp.float32)
+            )
+        return carry
+
+    lax.fori_loop(0, EXPERTS, gather, 0)
+
+
+def moe(packed, gate_weight, up_weight, down_weight, n):
+    model_width, width = gate_weight.shape
+    row_count = n * CAP
+    chunk = min(256, width)
+    piece = model_width // 4
+    pair_slots = min(5, width // chunk)
+    down_slots = min(3, model_width // piece)
+    anywhere = pl.BlockSpec(memory_space=pl.ANY)
+    whole = pl.BlockSpec(memory_space=pltpu.VMEM)
+    bf16, f32 = jnp.bfloat16, jnp.float32
+    return pl.pallas_call(
+        functools.partial(moe_kernel, n, n // EXPERTS, pair_slots, down_slots),
+        out_shape=jax.ShapeDtypeStruct((EXPERTS, CAP, model_width), f32),
+        in_specs=[whole, anywhere, anywhere, anywhere],
+        out_specs=whole,
+        scratch_shapes=[
+            pltpu.VMEM((pair_slots, model_width, chunk), bf16),
+            pltpu.VMEM((pair_slots, model_width, chunk), bf16),
+            pltpu.VMEM((down_slots, width, piece), bf16),
+            pltpu.VMEM((n, CAP, model_width), bf16),
+            pltpu.VMEM((row_count, model_width), f32),
+            pltpu.VMEM((row_count, model_width), bf16),
+            pltpu.VMEM((row_count, width), bf16),
+            pltpu.VMEM((row_count, piece), f32),
+            pltpu.VMEM((n, model_width // piece, CAP, piece), bf16),
+            pltpu.VMEM((n, model_width // piece, CAP, piece), bf16),
+            pltpu.SemaphoreType.DMA((2, pair_slots)),
+            pltpu.SemaphoreType.DMA((down_slots,)),
+            pltpu.SemaphoreType.DMA((n,)),
+            pltpu.SemaphoreType.DMA((n,)),
+            pltpu.SemaphoreType.DMA((n,)),
+            pltpu.SemaphoreType.DMA((n,)),
+            pltpu.SemaphoreType.DMA,
+        ],
+        compiler_params=pltpu.CompilerParams(
+            collective_id=0, has_side_effects=True, vmem_limit_bytes=VMEM_LIMIT
+        ),
+        name="moe",
+    )(packed, gate_weight, up_weight, down_weight)
+
+
+def draft_kernel(
+    n,
+    share,
+    piece,
+    blocks,
+    fc_hbm,
+    out,
+    fc_buf,
+    arrived,
+    rows_wide,
+    result,
+    leaving,
+    returned,
+    fc_sem,
+    out_sem,
+    in_sem,
+    back_out_sem,
+    back_in_sem,
+):
+    me = lax.axis_index("expert")
+    piece_count = fc_hbm.shape[1] // piece
+
+    def fc_copy(i):
+        cols = pl.ds(pl.multiple_of(i * piece, piece), piece)
+        return pltpu.make_async_copy(fc_hbm.at[:, cols], fc_buf.at[i], fc_sem.at[i])
+
+    def start_fc(i, carry):
+        fc_copy(i).start()
+        return carry
+
+    lax.fori_loop(0, piece_count, start_fc, 0)
+    greet(n, me)
+
+    def dispatch(k, carry):
+        peer = lax.rem(me + k, n)
+        push(blocks.at[peer], arrived.at[me], out_sem.at[peer], in_sem.at[me], peer).start()
+        return carry
+
+    lax.fori_loop(1, n, dispatch, 0)
+    rows_wide[pl.ds(me * share, share), :] = blocks[me]
+
+    def take(k, carry):
+        source = lax.rem(me + n - k, n)
+        push(
+            blocks.at[source], arrived.at[source], out_sem.at[source], in_sem.at[source], source
+        ).wait()
+        rows_wide[pl.ds(source * share, share), :] = arrived[source]
+        return carry
+
+    lax.fori_loop(1, n, take, 0)
+
+    def step(i, carry):
+        fc_copy(i).wait()
+        result[...] = jnp.dot(
+            rows_wide[...].astype(jnp.bfloat16), fc_buf[i], preferred_element_type=jnp.float32
+        )
+
+        def split(source, inner):
+            leaving[source, i] = result[pl.ds(source * share, share), :]
+            return inner
+
+        lax.fori_loop(0, n, split, 0)
+
+        def send_back(k, inner):
+            peer = lax.rem(me + k, n)
+            push(
+                leaving.at[peer, i],
+                returned.at[me, i],
+                back_out_sem.at[peer],
+                back_in_sem.at[me],
+                peer,
+            ).start()
+            return inner
+
+        lax.fori_loop(1, n, send_back, 0)
+        return carry
+
+    lax.fori_loop(0, piece_count, step, 0)
+    returned[me] = leaving[me]
+
+    def drain(k, carry):
+        peer = lax.rem(me + n - k, n)
+        push(
+            leaving.at[peer], returned.at[peer], back_out_sem.at[peer], back_in_sem.at[peer], peer
+        ).wait()
+        return carry
+
+    lax.fori_loop(1, n, drain, 0)
+    for i in range(piece_count):
+
+        def add(source, total):
+            return total + returned[source, i]
+
+        out[:, i * piece : (i + 1) * piece] = lax.fori_loop(
+            0, n, add, jnp.zeros((share, piece), jnp.float32)
+        ).astype(out.dtype)
+
+
+def draft(blocks, draft_fc):
+    n, share, depth = blocks.shape
+    model_width = draft_fc.shape[1]
+    piece = model_width // 4
+    pieces = model_width // piece
+    whole = pl.BlockSpec(memory_space=pltpu.VMEM)
+    f32 = jnp.float32
+    return pl.pallas_call(
+        functools.partial(draft_kernel, n, share, piece),
+        out_shape=jax.ShapeDtypeStruct((share, model_width), jnp.bfloat16),
+        in_specs=[whole, pl.BlockSpec(memory_space=pl.ANY)],
+        out_specs=whole,
+        scratch_shapes=[
+            pltpu.VMEM((pieces, depth, piece), jnp.bfloat16),
+            pltpu.VMEM((n, share, depth), f32),
+            pltpu.VMEM((n * share, depth), f32),
+            pltpu.VMEM((n * share, piece), f32),
+            pltpu.VMEM((n, pieces, share, piece), f32),
+            pltpu.VMEM((n, pieces, share, piece), f32),
+            pltpu.SemaphoreType.DMA((pieces,)),
+            pltpu.SemaphoreType.DMA((n,)),
+            pltpu.SemaphoreType.DMA((n,)),
+            pltpu.SemaphoreType.DMA((n,)),
+            pltpu.SemaphoreType.DMA((n,)),
+        ],
+        compiler_params=pltpu.CompilerParams(
+            collective_id=1, has_side_effects=True, vmem_limit_bytes=VMEM_LIMIT
+        ),
+        name="draft",
+    )(blocks, draft_fc)
 
 
 def per_device(
@@ -102,7 +469,6 @@
     draft_fc,
 ):
     devices = lax.axis_size("expert")
-    group_size = devices // EXPERTS
     context = attention(queries, tree_key_value, key_value_cache, lengths, parents)
     hidden_state = residual.astype(jnp.float32) + context
     normed = (
@@ -128,16 +494,7 @@
     packed = jnp.einsum(
         "ect,td->ecd", placing.astype(jnp.bfloat16), normed, preferred_element_type=jnp.float32
     ).astype(jnp.bfloat16)
-    outgoing = jnp.broadcast_to(packed[:, None], (EXPERTS, group_size, CAP, model_width)).reshape(
-        devices, CAP, model_width
-    )
-    received = lax.all_to_all(outgoing, "expert", split_axis=0, concat_axis=0, tiled=True)
-    flat_rows = received.reshape(-1, model_width)
-    computed = expert_rows(flat_rows, gate_weight, up_weight, down_weight).reshape(received.shape)
-    returned = lax.all_to_all(computed, "expert", split_axis=0, concat_axis=0, tiled=True)
-    grouped = jnp.sum(
-        returned.reshape(EXPERTS, group_size, CAP, model_width), axis=1, dtype=jnp.float32
-    )
+    grouped = moe(packed, gate_weight, up_weight, down_weight, devices)
     weighted = placing * mixing.T[:, None, :]
     expert_sum = jnp.einsum("ect,ecd->td", weighted, grouped, precision=lax.Precision.HIGHEST)
     layer_out = (hidden_state + expert_sum).astype(jnp.bfloat16)
@@ -152,13 +509,9 @@
         preferred_element_type=jnp.float32,
     ).astype(jnp.bfloat16)
     draft_in = jnp.concatenate([picked, next_embed], axis=1)
-    columns_in = lax.all_to_all(draft_in, "expert", split_axis=1, concat_axis=0, tiled=True)
-    draft_out = lax.psum_scatter(
-        jnp.dot(columns_in, draft_fc, preferred_element_type=jnp.float32),
-        "expert",
-        scatter_dimension=0,
-        tiled=True,
-    ).astype(jnp.bfloat16)
+    depth = draft_fc.shape[0]
+    blocks = draft_in.reshape(request_total, devices, depth).transpose(1, 0, 2)
+    draft_out = draft(blocks.astype(jnp.float32), draft_fc)
     return (layer_out, draft_out)
 
 

time: 184 us -> 99 us (0.54)
  blocking collectives: 88.8 us -> 0 us
  Pallas kernels: 0 us -> 75.2 us
  matrix products: 43.7 us -> 9.87 us
  waiting for transfers between devices: 23.8 us -> 0 us
  starting transfers between devices: 9.31 us -> 0 us
  local copies, waits for them, and re-layouts: 10.5 us -> 6.97 us
    pallas_call x0 -> x2, Pallas kernels: none -> 75.2 us  [the longest x1 52.7 us: moe(): pl.pallas_call(functools.partial(moe_kernel, n, n // EXPERTS, pair_slots,...]
    unnamed x1 -> x0, blocking collectives: 61.5 us -> none
    dot_general x3 -> x0, matrix products: 35.5 us -> none  [the longest x1 20 us: expert_rows(): jnp.dot(activation, down_weight, preferred_element_type=jnp.float32)]
    all_to_all x1 -> x0, blocking collectives: 27.3 us -> none  [per_device(): lax.all_to_all(outgoing, 'expert', split_axis=0, concat_axis=0, tiled=True)]
    all_to_all x2 -> x0, waiting for transfers between devices: 23.8 us -> none  [the longest x1 17.9 us: per_device(): lax.all_to_all(computed, 'expert', split_axis=0, concat_axis=0, tiled=True)]
    all_to_all x2 -> x0, starting transfers between devices: 9.31 us -> none  [the longest x1 5.38 us: per_device(): lax.all_to_all(draft_in, 'expert', split_axis=1, concat_axis=0, tiled=True)]
  transfers between devices with their start and end apart: 2 -> 0, of which waited for: 2 -> 0; matrix products, arithmetic and copies ran while one was open for 0% -> 0% of each run, Pallas kernels for 0% -> 0%
where the time goes in v1:
time: 99 us; the launch traced here: 98.3 us
  Pallas kernels  75.2 us (76%)
  matrix products  9.87 us (10%)
  local copies, waits for them, and re-layouts  6.97 us (7%)
  other arithmetic  4.12 us (4%)
  between operations  2.13 us (2%)
    pallas_call x1, Pallas kernels, moe(): pl.pallas_call(functools.partial(moe_kernel, n, n // EXPERTS, pair_slots,...  52.7 us
    pallas_call x1, Pallas kernels, draft(): pl.pallas_call(functools.partial(draft_kernel, n, share, piece), out_shap...  22.5 us
    dot_general x6, matrix products, ancestors(): jnp.einsum('rij,rjk->rik', current, parent_map, precision=lax.Precision.H...  5.08 us
    unnamed x13, local copies, waits for them, and re-layouts  2.49 us

profile of v1, /device:TPU:0, one launch (start us, length us, event | category | flops | bytes accessed | tf_op | source)
XLA Modules:
  0.0 98.3 jit_solution(9666913950579254612)
XLA Ops:
  0.6 0.0 copy-start
  0.6 0.9 fusion.26
  1.5 0.8 fusion.25
  2.3 0.8 fusion.24
  3.2 0.8 fusion.23
  4.0 0.8 fusion.22
  4.9 0.8 fusion.5
  5.7 1.0 %reshape.367 = bf16[6,8,6,128]{3,2,1,0:T(8,128)(2,1)S(1)} reshape(bf16[6,6144]{1,0:T(8,128)(2,1)} %param.15) | data formatting | bytes 147456 | tf_op jit(solution)/shard_map/reshape.2
  6.7 0.9 slice_reduce_fusion
  7.7 0.6 fusion.41
  8.2 1.7 %fusion.39 = (bf16[1,1,512,1024]{3,2,1,0:T(8,128)(2,1)S(1)}, bf16[1,1,512,1024]{3,2,1,0:T(8,128)(2,1)S(1)}) fusion(bf16[1,2,512,1024]{3,2,1,0:T(8,128)(2,1)} %param.17), kind=kLoop, calls=%fused_computation.78 | loop fusion | bytes 4194304 | tf_op jit(solution)/shard_map/slice | solution.py:41
  10.0 0.5 copy.46
  11.2 0.4 fusion.40
  11.6 0.1 fusion.10
  11.7 0.3 fusion.6
  12.0 0.2 fusion.12
  12.2 0.5 copy.47
  12.8 0.5 fusion.4
  13.4 1.1 %multiply_reduce_fusion = f32[6]{0:T(128)S(1)} fusion(f32[6,6144]{1,0:T(8,128)S(1)} %reshape.372, bf16[6,6144]{1,0:T(8,128)(2,1)} %param.20), kind=kLoop, calls=%fused_computation.19 | loop fusion | flops 147450 | bytes 221208 | tf_op jit(solution)/shard_map/reduce_sum | solution.py:476
  14.5 0.7 convert_element_type.71
  15.2 1.0 multiply_convert_fusion
  16.2 0.8 slice_bitcast_fusion.1
  16.9 0.2 select_reduce_fusion
  17.1 0.2 reduce_window_sum.11
  17.3 0.9 convolution_convert_fusion.packed
  18.2 52.7 %moe.1 = f32[4,4,6144]{2,1,0:T(4,128)} custom-call(bf16[4,4,6144]{2,1,0:T(4,128)(2,1)} %convolution_convert_fusion.packed, bf16[6144,2048]{1,0:T(8,128)(2,1)} %gate_hbm.1, bf16[6144,2048]{1,0:T(8,128)(2,1)} %up_hbm.1, bf16[2048,6144]{1,0:T(8,128)(2,1)} %down_hbm.1), custom_call_target="tpu_custom_call" | custom-call | tf_op jit(solution)/shard_map/moe/pallas_call | solution.py:293
  70.9 1.9 %fusion.1 = bf16[6,6144]{1,0:T(8,128)(2,1)S(1)} fusion(f32[4,4,6144]{2,1,0:T(4,128)} %moe.1, f32[6,6144]{1,0:T(8,128)S(1)} %reshape.372, bf16[6,6144]{1,0:T(8,128)(2,1)S(1)} %copy-done.1, f32[4,6]{1,0:T(4,128)S(1)} %get-tuple-element.10, f32[4,6]{1,0:T(4,128)S(1)} %get-tuple-element.11, f32[4,6]{1,0:T(4,128)S(1)} %add_bitcast_fusion), kind=kOutput, calls=%fused_computation.3 | convolution fusion | flops 7225632 | bytes 688416 | tf_op jit(solution)/shard_map/ect,ecd->td/dot_general | solution.py:499
  73.5 0.1 fusion.33
  73.7 0.1 pad_maximum_fusion
  73.7 0.7 convert.1.blocks
  74.4 22.5 %draft.1 = bf16[1,6144]{1,0:T(2,128)(2,1)} custom-call(f32[16,1,768]{2,1,0:T(1,128)} %convert.1.blocks, bf16[768,6144]{1,0:T(8,128)(2,1)} %fc_hbm.1), custom_call_target="tpu_custom_call" | custom-call | tf_op jit(solution)/shard_map/draft/pallas_call | solution.py:429
  96.9 1.4 %copy.75 = bf16[1,6144]{1,0:T(2,128)(2,1)} copy(bf16[1,6144]{1,0:T(2,128)(2,1)} %draft.1) | data formatting | bytes 24576
  (21 shorter events, 0.2 us)
Async XLA Ops:
  0.6 16.3 %copy-start = (bf16[6144,4]{0,1:T(4,128)(2,1)S(1)}, bf16[6144,4]{0,1:T(4,128)(2,1)}, u32[]{:S(2)}) copy-start(bf16[6144,4]{0,1:T(4,128)(2,1)} %param.22) | copy-start | bytes 147460
  18.2 52.7 %copy-start.1 = (bf16[6,6144]{1,0:T(8,128)(2,1)S(1)}, bf16[6,6144]{1,0:T(8,128)(2,1)}, u32[]{:S(2)}) copy-start(bf16[6,6144]{1,0:T(8,128)(2,1)} %param.20) | copy-start | bytes 221188
  18.2 55.5 %copy-start.3 = (bf16[1,6144]{1,0:T(2,128)(2,1)S(1)}, bf16[1,6144]{1,0:T(2,128)(2,1)}, u32[]{:S(2)}) copy-start(bf16[1,6144]{1,0:T(2,128)(2,1)} %param.28) | copy-start | bytes 36868
  72.8 25.5 %copy-start.2 = (bf16[6,6144]{1,0:T(8,128)(2,1)}, bf16[6,6144]{1,0:T(8,128)(2,1)S(1)}, u32[]{:S(2)}) copy-start(bf16[6,6144]{1,0:T(8,128)(2,1)S(1)} %fusion.1) | copy-start | bytes 221188

commit v2 on v1

--- a/solution.py
+++ b/solution.py
@@ -19,15 +19,28 @@
 EPSILON = 1e-05
 
 
+def related_kernel(parents, out):
+    node_ids = lax.broadcasted_iota(jnp.int32, (1, out.shape[2]), 1)
+    for request in range(out.shape[0]):
+        reached = []
+        for node in range(TREE_NODES):
+            row = (node_ids == node).astype(jnp.float32)
+            parent = parents[request * TREE_NODES + node]
+            for earlier in range(node):
+                row = row + jnp.where(parent == earlier, reached[earlier], 0.0)
+            reached.append(row)
+            out[request, node : node + 1, :] = row
+
+
 def ancestors(parent_ids):
-    node_ids = jnp.arange(TREE_NODES, dtype=jnp.int32)
-    parent_map = (parent_ids[:, :, None] == node_ids[None, None, :]).astype(jnp.float32)
-    current = jnp.broadcast_to(jnp.eye(TREE_NODES, dtype=jnp.float32), parent_map.shape)
-    reached = current
-    for repeat in range(TREE_NODES):
-        current = jnp.einsum("rij,rjk->rik", current, parent_map, precision=lax.Precision.HIGHEST)
-        reached = reached + current
-    return reached > 0.5
+    table = pl.pallas_call(
+        related_kernel,
+        out_shape=jax.ShapeDtypeStruct((parent_ids.shape[0] // TREE_NODES, TREE_NODES, 128), jnp.float32),
+        in_specs=[pl.BlockSpec(memory_space=pltpu.SMEM)],
+        out_specs=pl.BlockSpec(memory_space=pltpu.VMEM),
+        name="related",
+    )(parent_ids)
+    return table[:, :, :TREE_NODES] > 0.5
 
 
 def attention(queries, tree_key_value, key_value_cache, lengths, parents):
@@ -64,7 +77,7 @@
         * score_scale
     )
     visible = jnp.arange(CACHE_SLOTS, dtype=jnp.int32)[None, :] < lengths[:, None]
-    related = ancestors(parents.reshape(request_total, TREE_NODES))
+    related = ancestors(parents)
     cache_scores = jnp.where(visible[:, None, None, None, :], cache_scores, -1e30)
     tree_scores = jnp.where(related[:, None, :, None, :], tree_scores, -1e30)
     row_peak = jnp.maximum(jnp.max(cache_scores, axis=-1), jnp.max(tree_scores, axis=-1))[..., None]
@@ -283,10 +296,10 @@
 def moe(packed, gate_weight, up_weight, down_weight, n):
     model_width, width = gate_weight.shape
     row_count = n * CAP
-    chunk = min(256, width)
+    chunk = min(512, width)
     piece = model_width // 4
-    pair_slots = min(5, width // chunk)
-    down_slots = min(3, model_width // piece)
+    pair_slots = min(3, width // chunk)
+    down_slots = min(2, model_width // piece)
     anywhere = pl.BlockSpec(memory_space=pl.ANY)
     whole = pl.BlockSpec(memory_space=pltpu.VMEM)
     bf16, f32 = jnp.bfloat16, jnp.float32
@@ -342,6 +355,7 @@
 ):
     me = lax.axis_index("expert")
     piece_count = fc_hbm.shape[1] // piece
+    half = piece // 2
 
     def fc_copy(i):
         cols = pl.ds(pl.multiple_of(i * piece, piece), piece)
@@ -379,7 +393,10 @@
         )
 
         def split(source, inner):
-            leaving[source, i] = result[pl.ds(source * share, share), :]
+            block = result[pl.ds(source * share, share), :]
+            leaving[source, i] = jnp.concatenate(
+                [block[:, :half], block[:, half:]], axis=0
+            ).astype(jnp.bfloat16)
             return inner
 
         lax.fori_loop(0, n, split, 0)
@@ -412,11 +429,11 @@
     for i in range(piece_count):
 
         def add(source, total):
-            return total + returned[source, i]
-
-        out[:, i * piece : (i + 1) * piece] = lax.fori_loop(
-            0, n, add, jnp.zeros((share, piece), jnp.float32)
-        ).astype(out.dtype)
+            return total + returned[source, i].astype(jnp.float32)
+
+        total = lax.fori_loop(0, n, add, jnp.zeros((2 * share, half), jnp.float32))
+        out[:, i * piece : i * piece + half] = total[:share]
+        out[:, i * piece + half : (i + 1) * piece] = total[share:]
 
 
 def draft(blocks, draft_fc):
@@ -428,7 +445,7 @@
     f32 = jnp.float32
     return pl.pallas_call(
         functools.partial(draft_kernel, n, share, piece),
-        out_shape=jax.ShapeDtypeStruct((share, model_width), jnp.bfloat16),
+        out_shape=jax.ShapeDtypeStruct((share, model_width), f32),
         in_specs=[whole, pl.BlockSpec(memory_space=pl.ANY)],
         out_specs=whole,
         scratch_shapes=[
@@ -436,8 +453,8 @@
             pltpu.VMEM((n, share, depth), f32),
             pltpu.VMEM((n * share, depth), f32),
             pltpu.VMEM((n * share, piece), f32),
-            pltpu.VMEM((n, pieces, share, piece), f32),
-            pltpu.VMEM((n, pieces, share, piece), f32),
+            pltpu.VMEM((n, pieces, 2 * share, piece // 2), jnp.bfloat16),
+            pltpu.VMEM((n, pieces, 2 * share, piece // 2), jnp.bfloat16),
             pltpu.SemaphoreType.DMA((pieces,)),
             pltpu.SemaphoreType.DMA((n,)),
             pltpu.SemaphoreType.DMA((n,)),
@@ -511,7 +528,7 @@
     draft_in = jnp.concatenate([picked, next_embed], axis=1)
     depth = draft_fc.shape[0]
     blocks = draft_in.reshape(request_total, devices, depth).transpose(1, 0, 2)
-    draft_out = draft(blocks.astype(jnp.float32), draft_fc)
+    draft_out = draft(blocks.astype(jnp.float32), draft_fc).astype(jnp.bfloat16)
     return (layer_out, draft_out)
 
 

time: 99 us -> 91.4 us (0.923)
  matrix products: 9.87 us -> 4.79 us
  Pallas kernels: 75.2 us -> 72 us
  other arithmetic: 4.12 us -> 6.17 us
  local copies, waits for them, and re-layouts: 6.97 us -> 5.61 us
    dot_general x6 -> x0, matrix products: 5.08 us -> none  [ancestors(): jnp.einsum('rij,rjk->rik', current, parent_map, precision=lax.Precision.H...]
    pallas_call x1, Pallas kernels: 22.5 us -> 18.7 us  [draft(): pl.pallas_call(functools.partial(draft_kernel, n, share, piece), out_shap...]
    unnamed x13 -> x12, local copies, waits for them, and re-layouts: 2.49 us -> 1.12 us
    convert_element_type x1 -> x2, other arithmetic: 0.67 us -> 2.03 us  [per_device(): draft_out = draft(blocks.astype(jnp.float32), draft_fc).astype(jnp.bfloat16)]
    pallas_call x0 -> x1, Pallas kernels: none -> 1.28 us  [ancestors(): pl.pallas_call(related_kernel, out_shape=jax.ShapeDtypeStruct((parent_ids...]
where the time goes in v2:
time: 91.4 us; the launch traced here: 90.7 us
  Pallas kernels  72 us (79%)
  other arithmetic  6.17 us (7%)
  local copies, waits for them, and re-layouts  5.61 us (6%)
  matrix products  4.79 us (5%)
  between operations  2.13 us (2%)
    pallas_call x1, Pallas kernels, moe(): pl.pallas_call(functools.partial(moe_kernel, n, n // EXPERTS, pair_slots,...  52 us
    pallas_call x1, Pallas kernels, draft(): pl.pallas_call(functools.partial(draft_kernel, n, share, piece), out_shap...  18.7 us
    convert_element_type x2, other arithmetic, per_device(): draft_out = draft(blocks.astype(jnp.float32), draft_fc).astype(jnp.bfloat16)  2.03 us
    dot_general x1, matrix products, per_device(): jnp.einsum('ect,ecd->td', weighted, grouped, precision=lax.Precision.HIGH...  1.88 us

profile of v2, /device:TPU:0, one launch (start us, length us, event | category | flops | bytes accessed | tf_op | source)
XLA Modules:
  0.0 90.7 jit_solution(3661812183383402705)
XLA Ops:
  0.6 0.0 copy-start
  0.6 1.7 %fusion.28 = (bf16[1,1,512,1024]{3,2,1,0:T(8,128)(2,1)S(1)}, bf16[1,1,512,1024]{3,2,1,0:T(8,128)(2,1)S(1)}) fusion(bf16[1,2,512,1024]{3,2,1,0:T(8,128)(2,1)} %param.17), kind=kLoop, calls=%fused_computation.65 | loop fusion | bytes 4194304 | tf_op jit(solution)/shard_map/slice | solution.py:54
  2.4 0.5 copy.46
  2.9 1.0 %reshape.253 = bf16[6,8,6,128]{3,2,1,0:T(8,128)(2,1)S(1)} reshape(bf16[6,6144]{1,0:T(8,128)(2,1)} %param.15) | data formatting | bytes 147456 | tf_op jit(solution)/shard_map/reshape.2
  4.6 0.4 fusion.29
  5.0 0.9 %slice_reduce_fusion = (bf16[6,1024]{1,0:T(8,128)(2,1)S(1)}, bf16[6,1024]{1,0:T(8,128)(2,1)S(1)}) fusion(bf16[6,2,1024]{2,1,0:T(2,128)(2,1)} %param.16), kind=kLoop, calls=%fused_computation.27 | loop fusion | bytes 49152 | tf_op jit(solution)/shard_map/slice | solution.py:60
  5.9 1.3 %related.1 = f32[1,6,128]{2,1,0:T(8,128)} custom-call(s32[6]{0:T(128)} %parents.1), custom_call_target="tpu_custom_call" | custom-call | tf_op jit(solution)/shard_map/related/pallas_call | solution.py:36
  7.2 0.7 fusion.21
  7.9 0.6 fusion.30
  8.5 0.1 fusion.9
  8.6 0.3 fusion.5
  8.9 0.2 fusion.11
  9.1 0.5 copy.47
  9.7 0.5 fusion.4
  10.3 1.1 %multiply_reduce_fusion = f32[6]{0:T(128)S(1)} fusion(f32[6,6144]{1,0:T(8,128)S(1)} %reshape.258, bf16[6,6144]{1,0:T(8,128)(2,1)} %param.20), kind=kLoop, calls=%fused_computation.17 | loop fusion | flops 147450 | bytes 221208 | tf_op jit(solution)/shard_map/reduce_sum | solution.py:493
  11.4 0.7 convert_element_type.69
  12.1 1.0 %multiply_convert_fusion = bf16[6,6144]{1,0:T(8,128)(2,1)S(1)} fusion(f32[6144]{0:T(1024)S(1)} %convert_element_type.69, f32[6]{0:T(128)S(1)} %add_rsqrt_fusion, f32[6,6144]{1,0:T(8,128)S(1)} %reshape.258, bf16[6,6144]{1,0:T(8,128)(2,1)} %param.20), kind=kLoop, calls=%fused_computation.16 | loop fusion | flops 184320 | bytes 319512 | tf_op jit(solution)/shard_map/convert_element_type | solution.py:495
  13.1 0.8 slice_bitcast_fusion.1
  13.8 0.0 copy-done
  13.8 0.2 select_reduce_fusion
  14.0 0.2 reduce_window_sum.11
  14.2 0.9 convolution_convert_fusion.packed
  15.1 52.0 %moe.1 = f32[4,4,6144]{2,1,0:T(4,128)} custom-call(bf16[4,4,6144]{2,1,0:T(4,128)(2,1)} %convolution_convert_fusion.packed, bf16[6144,2048]{1,0:T(8,128)(2,1)} %gate_hbm.1, bf16[6144,2048]{1,0:T(8,128)(2,1)} %up_hbm.1, bf16[2048,6144]{1,0:T(8,128)(2,1)} %down_hbm.1), custom_call_target="tpu_custom_call" | custom-call | tf_op jit(solution)/shard_map/moe/pallas_call | solution.py:306
  67.1 0.0 copy-done.1
  67.2 1.9 %fusion.1 = bf16[6,6144]{1,0:T(8,128)(2,1)S(1)} fusion(f32[4,4,6144]{2,1,0:T(4,128)} %moe.1, f32[6,6144]{1,0:T(8,128)S(1)} %reshape.258, bf16[6,6144]{1,0:T(8,128)(2,1)S(1)} %copy-done.1, f32[4,6]{1,0:T(4,128)S(1)} %get-tuple-element.10, f32[4,6]{1,0:T(4,128)S(1)} %get-tuple-element.11, f32[4,6]{1,0:T(4,128)S(1)} %add_bitcast_fusion), kind=kOutput, calls=%fused_computation.3 | convolution fusion | flops 7225632 | bytes 688416 | tf_op jit(solution)/shard_map/ect,ecd->td/dot_general | solution.py:516
  69.0 0.0 copy-start.2
  69.7 0.1 fusion.22
  69.9 0.0 copy-done.3
  69.9 0.1 pad_maximum_fusion
  70.0 0.7 convert.1.blocks
  70.6 18.7 %draft.1 = f32[1,6144]{1,0:T(1,128)} custom-call(f32[16,1,768]{2,1,0:T(1,128)} %convert.1.blocks, bf16[768,6144]{1,0:T(8,128)(2,1)} %fc_hbm.1), custom_call_target="tpu_custom_call" | custom-call | tf_op jit(solution)/shard_map/draft/pallas_call | solution.py:446
  89.4 1.4 %convert_element_type.78 = bf16[1,6144]{1,0:T(2,128)(2,1)} convert(f32[1,6144]{1,0:T(1,128)} %draft.1) | non-fusion elementwise | flops 6144 | bytes 36864 | tf_op jit(solution)/shard_map/convert_element_type | solution.py:531
  (17 shorter events, 0.2 us)
Async XLA Ops:
  0.6 13.2 %copy-start = (bf16[6144,4]{0,1:T(4,128)(2,1)S(1)}, bf16[6144,4]{0,1:T(4,128)(2,1)}, u32[]{:S(2)}) copy-start(bf16[6144,4]{0,1:T(4,128)(2,1)} %param.22) | copy-start | bytes 147460
  15.1 52.0 %copy-start.1 = (bf16[6,6144]{1,0:T(8,128)(2,1)S(1)}, bf16[6,6144]{1,0:T(8,128)(2,1)}, u32[]{:S(2)}) copy-start(bf16[6,6144]{1,0:T(8,128)(2,1)} %param.20) | copy-start | bytes 221188
  15.1 54.8 %copy-start.3 = (bf16[1,6144]{1,0:T(2,128)(2,1)S(1)}, bf16[1,6144]{1,0:T(2,128)(2,1)}, u32[]{:S(2)}) copy-start(bf16[1,6144]{1,0:T(2,128)(2,1)} %param.28) | copy-start | bytes 36868
  69.0 21.7 %copy-start.2 = (bf16[6,6144]{1,0:T(8,128)(2,1)}, bf16[6,6144]{1,0:T(8,128)(2,1)S(1)}, u32[]{:S(2)}) copy-start(bf16[6,6144]{1,0:T(8,128)(2,1)S(1)} %fusion.1) | copy-start | bytes 221188
